TPU v7x, 32 devices: a whole 2x2x4 slice. The times are simulated.
32 devices in a mesh: gx: 2 (over x), gy: 16 (over z, y, core).
Axes of the slice: x: 2, y: 2, z: 4, core: 2. Of those that a mesh axis runs over, the one named last changes fastest.
Arguments:
- concentration: float32 [64, 256, 256], P('gx', 'gy'), may hold values from 0.1 to 4
- face_conductance: float32 [64, 256, 256], P('gx', 'gy'), may hold values from 3 to 1000
- release: float32 [64, 256, 256], P('gx', 'gy'), may hold values from 0.1 to 1
- trap_rate: float32 [64, 256, 256], P('gx', 'gy'), may hold values from 0.5 to 2
Outputs:
- final_concentration: float32 [64, 256, 256], P('gx', 'gy')
All inputs are finite; a program needn't handle non-finite values.
Results may differ from a plain program's by a relative error of at most 0.0003.
Values sent between devices are 32-bit elements; how exact they have to be, the bound alone decides.
A program may use at most 64 MiB of HBM per device.

v0:
```python
import jax
import jax.numpy as jnp
from jax import lax
from jax.experimental import pallas as pl
from jax.experimental.pallas import tpu as pltpu
from jax.sharding import PartitionSpec as P

STEPS = 2
SUBSTEPS = 4


y_weight = 0.32
z_weight = 0.16
time_step = 0.25


def shifted(value, axis, by):
    peers = lax.axis_size(axis)
    pairs = [(i, i + by) for i in range(peers) if 0 <= i + by < peers]
    return lax.ppermute(value, axis, pairs)


def extended_2(block, sides, width):
    for axis, dim in sides:
        count = lax.axis_size(axis)
        forward = [(i, i + 1) for i in range(count - 1)]
        backward = [(target, source) for source, target in forward]
        low = lax.ppermute(
            lax.slice_in_dim(block, block.shape[dim] - width, None, axis=dim), axis, forward
        )
        high = lax.ppermute(lax.slice_in_dim(block, 0, width, axis=dim), axis, backward)
        block = jnp.concatenate([low, block, high], axis=dim)
    return block


def thomas(lower, middle, upper, right):

    def forward(carry, row):
        factor_prev, value_prev = carry
        below_row, main_row, above_row, right_row = row
        divisor = main_row - below_row * factor_prev
        factor = above_row / divisor
        scaled = (right_row - below_row[None] * value_prev) / divisor[None]
        return ((factor, scaled), (factor, scaled))

    start = (jnp.zeros_like(middle[0]), jnp.zeros_like(right[0]))
    unused, (factors, scaled) = lax.scan(forward, start, (lower, middle, upper, right))

    def backward(following, row):
        factor, value = row
        current = value - factor[None] * following
        return (current, current)

    unused, values = lax.scan(backward, jnp.zeros_like(right[0]), (factors, scaled), reverse=True)
    return values


def advance(center, below, above, release, trap_rate):
    left = jnp.concatenate([center[:, :, :1], center[:, :, :-1]], axis=2)
    right = jnp.concatenate([center[:, :, 1:], center[:, :, -1:]], axis=2)
    square = center * center
    reaction = release - trap_rate * square / (1.0 + square)
    return (
        center
        + y_weight * (above + below - 2.0 * center)
        + z_weight * (left + right - 2.0 * center)
        + time_step * reaction
    )


def line_section(field, faces_used):
    rows_x = field.shape[0]
    blank = jnp.zeros_like(faces_used[:1])
    lower = jnp.concatenate([blank, -faces_used[1 : rows_x - 1]], axis=0)
    upper = jnp.concatenate([-faces_used[1 : rows_x - 1], blank], axis=0)
    middle = 1.0 + faces_used[:-1] + faces_used[1:]
    row_index = jnp.arange(rows_x - 1)[:, None, None]
    first_unit = jnp.where(row_index == 0, faces_used[0:1], jnp.float32(0.0))
    last_unit = jnp.where(
        row_index == rows_x - 2, faces_used[rows_x - 1 : rows_x], jnp.float32(0.0)
    )
    right = jnp.stack([field[1:], first_unit, last_unit], axis=1)
    solved = thomas(lower, middle, upper, right)
    inner = solved[:, 0]
    left_part = solved[:, 1]
    right_part = solved[:, 2]
    edge = jnp.stack([faces_used[-1], inner[-1], left_part[-1], right_part[-1]])
    came = shifted(edge, "gx", 1)
    prior_face = came[0]
    own_face = faces_used[0]
    coef_lower = -prior_face * came[2]
    coef_main = 1.0 + prior_face + own_face - prior_face * came[3] - own_face * left_part[0]
    coef_upper = -own_face * right_part[0]
    coef_right = field[0] + prior_face * came[1] + own_face * inner[0]
    system = jnp.stack([coef_lower, coef_main, coef_upper, coef_right])[:, None]
    whole = lax.all_gather(system, "gx", axis=1, tiled=True)
    firsts = thomas(whole[0], whole[1], whole[2], whole[3][:, None])[:, 0]
    position = lax.axis_index("gx")
    count = lax.axis_size("gx")
    first = lax.dynamic_index_in_dim(firsts, position, 0, keepdims=False)
    following = lax.dynamic_index_in_dim(
        firsts, jnp.minimum(position + 1, count - 1), 0, keepdims=False
    )
    rest = inner + first[None] * left_part + following[None] * right_part
    return jnp.concatenate([first[None], rest], axis=0)


def local(concentration, face_conductance, release, trap_rate):
    rows_x = concentration.shape[0]
    rows_y = concentration.shape[1]
    is_last = lax.axis_index("gx") == lax.axis_size("gx") - 1
    inside = jnp.logical_or(
        jnp.arange(rows_x)[:, None, None] < rows_x - 1, jnp.logical_not(is_last)
    )
    faces_used = jnp.where(inside, face_conductance, jnp.float32(0.0))
    field = concentration
    margin = SUBSTEPS
    rates = extended_2(jnp.stack([release, trap_rate]), (("gy", 2),), margin)
    global_rows = lax.axis_index("gy") * rows_y - margin + jnp.arange(rows_y + 2 * margin)
    valid = jnp.logical_and(global_rows >= 0, global_rows < lax.axis_size("gy") * rows_y)
    for step in range(STEPS):
        field = line_section(field, faces_used)
        extended = extended_2(field, (("gy", 1),), margin)
        for substep in range(SUBSTEPS):
            span = extended.shape[1] - 2
            offset = substep + 1
            source_part = rates[0][:, offset : offset + span]
            trap_part = rates[1][:, offset : offset + span]
            keeping = valid[offset : offset + span][None, :, None]
            updated = advance(
                extended[:, 1:-1], extended[:, :-2], extended[:, 2:], source_part, trap_part
            )
            extended = jnp.where(keeping, updated, jnp.float32(0.0))
        field = extended
    return field


SUB = 8
LANES = 128
VMEM_LIMIT = 67_043_328
MESH = pl.DeviceIdType.MESH


def inverse(value):
    return 1.0 / value


def kernel(
    c_hbm, f_hbm, rel_hbm, trap_hbm, out_hbm,
    c_in, f_in, rel_in, trap_in, factor, scale, partial, solved,
    rates, wide, ping, pong, edge_out, edge_got,
    load_sem, store_sem, edge_send, edge_recv, rate_send, rate_recv, halo_send, halo_recv,
):
    blocks, planes, rows, lanes = c_in.shape
    chunks = planes // SUB
    halo = SUBSTEPS
    reach = SUBSTEPS - 1
    side = lax.axis_index("gx")
    spot = lax.axis_index("gy")
    count = lax.axis_size("gy")
    has_prev = spot > 0
    has_next = spot < count - 1
    partner = {"gx": 1 - side}
    to_next = {"gy": jnp.minimum(spot + 1, count - 1)}
    to_prev = {"gy": jnp.maximum(spot - 1, 0)}
    every = range(blocks)

    loads = []
    for n, (src, dst) in enumerate(
        ((rel_hbm, rel_in), (trap_hbm, trap_in), (f_hbm, f_in), (c_hbm, c_in))
    ):
        loads.append([
            pltpu.make_async_copy(
                src.at[:, :, pl.ds(b * lanes, lanes)], dst.at[b], load_sem.at[n, b]
            )
            for b in every
        ])
    for load in loads:
        for part in load:
            part.start()

    barrier = pltpu.get_barrier_semaphore()
    pl.semaphore_signal(barrier, inc=1, device_id=partner, device_id_type=MESH)

    @pl.when(has_next)
    def _():
        pl.semaphore_signal(barrier, inc=1, device_id=to_next, device_id_type=MESH)

    @pl.when(has_prev)
    def _():
        pl.semaphore_signal(barrier, inc=1, device_id=to_prev, device_id_type=MESH)

    def remote(src, dst, send, recv, target):
        return pltpu.make_async_remote_copy(
            src_ref=src, dst_ref=dst, send_sem=send, recv_sem=recv,
            device_id=target, device_id_type=MESH,
        )

    rate_copies = (
        remote(
            rates.at[:, pl.ds(rows, reach)], rates.at[:, pl.ds(0, reach)],
            rate_send.at[0], rate_recv.at[0], to_next,
        ),
        remote(
            rates.at[:, pl.ds(reach, reach)], rates.at[:, pl.ds(rows + reach, reach)],
            rate_send.at[1], rate_recv.at[1], to_prev,
        ),
    )

    def chunk_of(k):
        return chunks - 1 - k + side * (2 * k - chunks + 1)

    def halo_copies(step, k):
        part = wide.at[step, chunk_of(k)]
        return (
            remote(
                part.at[pl.ds(rows, halo)], part.at[pl.ds(0, halo)],
                halo_send.at[step, k, 0], halo_recv.at[step, k, 0], to_next,
            ),
            remote(
                part.at[pl.ds(halo, halo)], part.at[pl.ds(rows + halo, halo)],
                halo_send.at[step, k, 1], halo_recv.at[step, k, 1], to_prev,
            ),
        )

    def start_two(first, second):
        @pl.when(has_next)
        def _():
            first.start()

        @pl.when(has_prev)
        def _():
            second.start()

    def got_two(first, second):
        @pl.when(has_prev)
        def _():
            first.wait_recv()

        @pl.when(has_next)
        def _():
            second.wait_recv()

    def sent_two(first, second):
        @pl.when(has_next)
        def _():
            first.wait_send()

        @pl.when(has_prev)
        def _():
            second.wait_send()

    def flat(ref, b):
        return ref.at[b].reshape(planes * rows, lanes)

    def across(group, y):
        return pl.ds(group * (SUB * rows) + y, SUB, stride=rows)

    for load in loads[:2]:
        for part in load:
            part.wait()

    def prepare(group, carry):
        for y in range(rows):
            for b in every:
                trap = time_step * flat(trap_in, b)[across(group, y), :]
                release = time_step * flat(rel_in, b)[across(group, y), :]
                rates[0, reach + y, group, b] = release - trap
                rates[1, reach + y, group, b] = trap
        return carry

    lax.fori_loop(0, chunks, prepare, 0)

    pl.semaphore_wait(barrier, 1 + has_prev.astype(jnp.int32) + has_next.astype(jnp.int32))
    start_two(*rate_copies)

    for load in loads[2:]:
        for part in load:
            part.wait()

    edge_copies = (
        remote(
            edge_out.at[pl.ds(0, 3)], edge_got.at[pl.ds(0, 3)],
            edge_send.at[0], edge_recv.at[0], partner,
        ),
        remote(edge_out.at[3], edge_got.at[3], edge_send.at[1], edge_recv.at[1], partner),
    )

    lane = lax.broadcasted_iota(jnp.int32, (SUB, lanes), 1)
    lane_first, lane_last = lane == 0, lane == lanes - 1

    def substep(inner, read, group, write):
        span = rows + 2 * (reach - inner)
        start = -(reach - inner)

        def clean(y, value):
            if y < 0:
                return jnp.where(has_prev, value, 0.0)
            if y >= rows:
                return jnp.where(has_next, value, 0.0)
            return value

        def fetch(y):
            got = [read(y, b) for b in every]
            return [clean(y, v) for v in got] if inner == 0 else got

        window = [fetch(start - 1), fetch(start)]
        for y in range(start, start + span):
            window.append(fetch(y + 1))
            above, center, below = window[-3:]
            window = window[-2:]
            right = [pltpu.roll(v, 1, axis=1) for v in center]
            left = [pltpu.roll(v, lanes - 1, axis=1) for v in center]
            for b in every:
                c = center[b]
                lower = jnp.where(lane_first, right[b - 1] if b > 0 else c, right[b])
                upper = jnp.where(lane_last, left[b + 1] if b < blocks - 1 else c, left[b])
                value = (
                    (1.0 - 2.0 * y_weight - 2.0 * z_weight) * c
                    + y_weight * (above[b] + below[b])
                    + z_weight * (lower + upper)
                    + (
                        rates[0, reach + y, group, b]
                        + rates[1, reach + y, group, b] * inverse(1.0 + c * c)
                    )
                )
                write(y, b, clean(y, value))

    def plane(ref, x):
        return [ref[b, x] for b in every]

    for step in range(STEPS):
        def position(i):
            return i + side * (planes - 1 - 2 * i)

        right = plane(c_in, position(0))
        if step == 0:
            main = [jnp.ones_like(v) for v in right]
        for i in range(planes - 1):
            if step == 0:
                face = plane(f_in, i + side * (planes - 2 - 2 * i))
                inv = [inverse(main[b] + face[b]) for b in every]
                ratio = [face[b] * inv[b] for b in every]
                for b in every:
                    factor[i, b] = ratio[b]
                    scale[i, b] = inv[b]
                main = [1.0 + ratio[b] * main[b] for b in every]
            else:
                ratio = [factor[i, b] for b in every]
                inv = [scale[i, b] for b in every]
            following = plane(c_in, position(i + 1))
            for b in every:
                partial[i, b] = right[b] * inv[b]
            right = [following[b] + ratio[b] * right[b] for b in every]
        if step == 0:
            for b in every:
                edge_out[0, b] = right[b]
                edge_out[1, b] = main[b]
                edge_out[2, b] = f_in[b, planes - 1]
            edge_copies[0].start()
            edge_copies[0].wait_recv()
            value = []
            for b in every:
                other = edge_got[1, b]
                face = jnp.where(side == 0, f_in[b, planes - 1], edge_got[2, b])
                inv = inverse(main[b] * other + face * (main[b] + other))
                own_weight = (other + face) * inv
                other_weight = face * inv
                value.append(own_weight * right[b] + other_weight * edge_got[0, b])
                edge_out[4, b] = own_weight
                edge_out[5, b] = other_weight
        else:
            for b in every:
                edge_out[3, b] = right[b]
            edge_copies[1].start()
            edge_copies[1].wait_recv()
            value = [
                edge_out[4, b] * right[b] + edge_out[5, b] * edge_got[3, b] for b in every
            ]
        for k in range(chunks):
            for i in reversed(range((chunks - 1 - k) * SUB, (chunks - k) * SUB)):
                if i < planes - 1:
                    value = [partial[i, b] + factor[i, b] * value[b] for b in every]
                for b in every:
                    solved[b, position(i)] = value[b]
            group = chunk_of(k)
            for y in range(rows):
                for b in every:
                    wide[step, group, halo + y, b] = flat(solved, b)[across(group, y), :]
            start_two(*halo_copies(step, k))
        if step == 0:
            got_two(*rate_copies)

        def finish(k, carry, step=step):
            group = chunk_of(k)
            got_two(*halo_copies(step, k))

            def first(y, b):
                return wide[step, group, halo + y, b]

            def reader(ref):
                return lambda y, b: ref[halo + y, b]

            def writer(ref):
                def put(y, b, value):
                    ref[halo + y, b] = value
                return put

            def last(y, b, value):
                flat(c_in, b)[across(group, y), :] = value

            read = first
            for inner in range(SUBSTEPS):
                target = (ping, pong)[inner % 2]
                write = last if inner == SUBSTEPS - 1 else writer(target)
                substep(inner, read, group, write)
                read = reader(target)
            if step == STEPS - 1:
                for b in every:
                    store(group, b).start()
            return carry

        def store(group, b):
            part = pl.ds(group * SUB, SUB)
            return pltpu.make_async_copy(
                c_in.at[b, part],
                out_hbm.at[part, :, pl.ds(b * lanes, lanes)],
                store_sem.at[group, b],
            )

        lax.fori_loop(0, chunks, finish, 0)

    for copy in edge_copies:
        copy.wait_send()
    sent_two(*rate_copies)
    for step in range(STEPS):
        for k in range(chunks):
            sent_two(*halo_copies(step, k))
    for group in range(chunks):
        for b in every:
            store(group, b).wait()


def fused(concentration, face_conductance, release, trap_rate):
    planes, rows, depth = concentration.shape
    blocks, chunks = depth // LANES, planes // SUB
    block = pltpu.VMEM((blocks, planes, rows, LANES), jnp.float32)
    kept = pltpu.VMEM((planes, blocks, rows, LANES), jnp.float32)
    edge = pltpu.VMEM((6, blocks, rows, LANES), jnp.float32)
    stage = pltpu.VMEM((rows + 2 * SUBSTEPS, blocks, SUB, LANES), jnp.float32)
    return pl.pallas_call(
        kernel,
        out_shape=jax.ShapeDtypeStruct((planes, rows, depth), jnp.float32),
        in_specs=[pl.BlockSpec(memory_space=pl.ANY)] * 4,
        out_specs=pl.BlockSpec(memory_space=pl.ANY),
        scratch_shapes=[block] * 4 + [kept] * 3 + [block] + [
            pltpu.VMEM(
                (2, rows + 2 * (SUBSTEPS - 1), chunks, blocks, SUB, LANES), jnp.float32
            ),
            pltpu.VMEM(
                (STEPS, chunks, rows + 2 * SUBSTEPS, blocks, SUB, LANES), jnp.float32
            ),
            stage, stage, edge, edge,
            pltpu.SemaphoreType.DMA((4, blocks)),
            pltpu.SemaphoreType.DMA((chunks, blocks)),
            pltpu.SemaphoreType.DMA((2,)),
            pltpu.SemaphoreType.DMA((2,)),
            pltpu.SemaphoreType.DMA((2,)),
            pltpu.SemaphoreType.DMA((2,)),
            pltpu.SemaphoreType.DMA((STEPS, chunks, 2)),
            pltpu.SemaphoreType.DMA((STEPS, chunks, 2)),
        ],
        compiler_params=pltpu.CompilerParams(
            collective_id=0, has_side_effects=True, vmem_limit_bytes=VMEM_LIMIT
        ),
    )(concentration, face_conductance, release, trap_rate)


def solution(mesh):
    placed = (P("gx", "gy", None), P("gx", "gy", None), P("gx", "gy", None), P("gx", "gy", None))

    def body(concentration, *rest):
        planes, rows, depth = concentration.shape
        fits = (
            mesh.shape["gx"] == 2
            and planes % SUB == 0
            and rows >= 2 * SUBSTEPS
            and rows % SUB == 0
            and depth % LANES == 0
        )
        return (fused if fits else local)(concentration, *rest)

    return jax.shard_map(
        body, mesh=mesh, in_specs=placed, out_specs=P("gx", "gy", None), check_vma=False
    )
```

profile of v0, /device:TPU:1, one launch (start us, length us, event | category | flops | bytes accessed | tf_op | source)
XLA Modules:
  0.0 22.8 jit_solution(702488280889060670)
XLA Ops:
  0.0 20.9 %shard_map.46 = f32[32,16,256]{2,1,0:T(8,128)} custom-call(f32[32,16,256]{2,1,0:T(8,128)} %c_hbm.1, f32[32,16,256]{2,1,0:T(8,128)} %f_hbm.1, f32[32,16,256]{2,1,0:T(8,128)} %rel_hbm.1, f32[32,16,256]{2,1,0:T(8,128)} %trap_hbm.1), custom_call_target="tpu_custom_call" | custom-call | tf_op jit(solution)/shard_map/pallas_call | solution.py:451
  20.9 1.9 %copy.6 = f32[32,16,256]{2,1,0:T(8,128)} copy(f32[32,16,256]{2,1,0:T(8,128)} %shard_map.46) | data formatting | bytes 1048576
where the time goes:
time: 23 us; the launch traced here: 22.8 us
  Pallas kernels  20.9 us (91%)
  local copies, waits for them, and re-layouts  1.87 us (8%)
    pallas_call x1, Pallas kernels, fused(): pl.pallas_call(kernel, out_shape=jax.ShapeDtypeStruct((planes, rows, dept...  20.9 us
    unnamed x1, local copies, waits for them, and re-layouts  1.87 us

commit v1 on v0

--- a/solution.py
+++ b/solution.py
@@ -148,7 +148,7 @@
 def kernel(
     c_hbm, f_hbm, rel_hbm, trap_hbm, out_hbm,
     c_in, f_in, rel_in, trap_in, factor, scale, partial, solved,
-    rates, wide, ping, pong, edge_out, edge_got,
+    rates, wide, levels, edge_out, edge_got,
     load_sem, store_sem, edge_send, edge_recv, rate_send, rate_recv, halo_send, halo_recv,
 ):
     blocks, planes, rows, lanes = c_in.shape
@@ -260,16 +260,19 @@
         for part in load:
             part.wait()
 
-    def prepare(group, carry):
-        for y in range(rows):
-            for b in every:
-                trap = time_step * flat(trap_in, b)[across(group, y), :]
-                release = time_step * flat(rel_in, b)[across(group, y), :]
-                rates[0, reach + y, group, b] = release - trap
-                rates[1, reach + y, group, b] = trap
-        return carry
-
-    lax.fori_loop(0, chunks, prepare, 0)
+    def prepare(spans):
+        def body(group, carry):
+            for y in [y for span in spans for y in span]:
+                for b in every:
+                    trap = time_step * flat(trap_in, b)[across(group, y), :]
+                    release = time_step * flat(rel_in, b)[across(group, y), :]
+                    rates[0, reach + y, group, b] = release - trap
+                    rates[1, reach + y, group, b] = trap
+            return carry
+
+        lax.fori_loop(0, chunks, body, 0)
+
+    prepare((range(reach), range(rows - reach, rows)))
 
     pl.semaphore_wait(barrier, 1 + has_prev.astype(jnp.int32) + has_next.astype(jnp.int32))
     start_two(*rate_copies)
@@ -289,9 +292,8 @@
     lane = lax.broadcasted_iota(jnp.int32, (SUB, lanes), 1)
     lane_first, lane_last = lane == 0, lane == lanes - 1
 
-    def substep(inner, read, group, write):
-        span = rows + 2 * (reach - inner)
-        start = -(reach - inner)
+    def substep(inner, span, read, group, write):
+        start = span[0]
 
         def clean(y, value):
             if y < 0:
@@ -305,7 +307,7 @@
             return [clean(y, v) for v in got] if inner == 0 else got
 
         window = [fetch(start - 1), fetch(start)]
-        for y in range(start, start + span):
+        for y in span:
             window.append(fetch(y + 1))
             above, center, below = window[-3:]
             window = window[-2:]
@@ -358,6 +360,7 @@
                 edge_out[1, b] = main[b]
                 edge_out[2, b] = f_in[b, planes - 1]
             edge_copies[0].start()
+            prepare((range(reach, rows - reach),))
             edge_copies[0].wait_recv()
             value = []
             for b in every:
@@ -388,33 +391,42 @@
                 for b in every:
                     wide[step, group, halo + y, b] = flat(solved, b)[across(group, y), :]
             start_two(*halo_copies(step, k))
-        if step == 0:
-            got_two(*rate_copies)
+
+        def run(group, spans_of, step=step):
+            def first(y, b):
+                return wide[step, group, halo + y, b]
+
+            def level(inner):
+                return lambda y, b: levels[inner, group, halo + y, b]
+
+            def keep(inner):
+                def put(y, b, value):
+                    levels[inner, group, halo + y, b] = value
+                return put
+
+            def last(y, b, value):
+                flat(c_in, b)[across(group, y), :] = value
+
+            for inner in range(SUBSTEPS):
+                for span in spans_of(inner):
+                    substep(
+                        inner, span,
+                        first if inner == 0 else level(inner - 1),
+                        group,
+                        last if inner == SUBSTEPS - 1 else keep(inner),
+                    )
+
+        def inside(k, carry):
+            run(chunk_of(k), lambda inner: (range(inner + 1, rows - 1 - inner),))
+            return carry
 
         def finish(k, carry, step=step):
             group = chunk_of(k)
             got_two(*halo_copies(step, k))
-
-            def first(y, b):
-                return wide[step, group, halo + y, b]
-
-            def reader(ref):
-                return lambda y, b: ref[halo + y, b]
-
-            def writer(ref):
-                def put(y, b, value):
-                    ref[halo + y, b] = value
-                return put
-
-            def last(y, b, value):
-                flat(c_in, b)[across(group, y), :] = value
-
-            read = first
-            for inner in range(SUBSTEPS):
-                target = (ping, pong)[inner % 2]
-                write = last if inner == SUBSTEPS - 1 else writer(target)
-                substep(inner, read, group, write)
-                read = reader(target)
+            run(group, lambda inner: (
+                range(inner - reach, inner + 1),
+                range(rows - 1 - inner, rows + reach - inner),
+            ))
             if step == STEPS - 1:
                 for b in every:
                     store(group, b).start()
@@ -428,6 +440,9 @@
                 store_sem.at[group, b],
             )
 
+        lax.fori_loop(0, chunks, inside, 0)
+        if step == 0:
+            got_two(*rate_copies)
         lax.fori_loop(0, chunks, finish, 0)
 
     for copy in edge_copies:
@@ -447,8 +462,10 @@
     block = pltpu.VMEM((blocks, planes, rows, LANES), jnp.float32)
     kept = pltpu.VMEM((planes, blocks, rows, LANES), jnp.float32)
     edge = pltpu.VMEM((6, blocks, rows, LANES), jnp.float32)
-    stage = pltpu.VMEM((rows + 2 * SUBSTEPS, blocks, SUB, LANES), jnp.float32)
-    return pl.pallas_call(
+    stage = pltpu.VMEM(
+        (SUBSTEPS - 1, chunks, rows + 2 * SUBSTEPS, blocks, SUB, LANES), jnp.float32
+    )
+    parts = pl.pallas_call(
         kernel,
         out_shape=jax.ShapeDtypeStruct((planes, rows, depth), jnp.float32),
         in_specs=[pl.BlockSpec(memory_space=pl.ANY)] * 4,
@@ -460,7 +477,7 @@
             pltpu.VMEM(
                 (STEPS, chunks, rows + 2 * SUBSTEPS, blocks, SUB, LANES), jnp.float32
             ),
-            stage, stage, edge, edge,
+            stage, edge, edge,
             pltpu.SemaphoreType.DMA((4, blocks)),
             pltpu.SemaphoreType.DMA((chunks, blocks)),
             pltpu.SemaphoreType.DMA((2,)),
@@ -474,6 +491,7 @@
             collective_id=0, has_side_effects=True, vmem_limit_bytes=VMEM_LIMIT
         ),
     )(concentration, face_conductance, release, trap_rate)
+    return parts
 
 
 def solution(mesh):

time: 23 us -> 22.5 us (0.978)
  Pallas kernels: 20.9 us -> 20.4 us
    pallas_call x1, Pallas kernels: 20.9 us -> 20.4 us  [fused(): pl.pallas_call(kernel, out_shape=jax.ShapeDtypeStruct((planes, rows, dept...]
where the time goes in v1:
time: 22.5 us; the launch traced here: 22.3 us
  Pallas kernels  20.4 us (91%)
  local copies, waits for them, and re-layouts  1.87 us (8%)
    pallas_call x1, Pallas kernels, fused(): pl.pallas_call(kernel, out_shape=jax.ShapeDtypeStruct((planes, rows, dept...  20.4 us
    unnamed x1, local copies, waits for them, and re-layouts  1.87 us

profile of v1, /device:TPU:1, one launch (start us, length us, event | category | flops | bytes accessed | tf_op | source)
XLA Modules:
  0.0 22.3 jit_solution(14766645086992929500)
XLA Ops:
  0.0 20.4 %shard_map.46 = f32[32,16,256]{2,1,0:T(8,128)} custom-call(f32[32,16,256]{2,1,0:T(8,128)} %c_hbm.1, f32[32,16,256]{2,1,0:T(8,128)} %f_hbm.1, f32[32,16,256]{2,1,0:T(8,128)} %rel_hbm.1, f32[32,16,256]{2,1,0:T(8,128)} %trap_hbm.1), custom_call_target="tpu_custom_call" | custom-call | tf_op jit(solution)/shard_map/pallas_call | solution.py:468
  20.4 1.9 %copy.6 = f32[32,16,256]{2,1,0:T(8,128)} copy(f32[32,16,256]{2,1,0:T(8,128)} %shard_map.46) | data formatting | bytes 1048576

commit v2 on v1

--- a/solution.py
+++ b/solution.py
@@ -137,7 +137,7 @@
 
 SUB = 8
 LANES = 128
-VMEM_LIMIT = 67_043_328
+VMEM_LIMIT = 67_043_328 - 1200 * 1024
 MESH = pl.DeviceIdType.MESH
 
 
@@ -146,10 +146,10 @@
 
 
 def kernel(
-    c_hbm, f_hbm, rel_hbm, trap_hbm, out_hbm,
+    c_hbm, f_hbm, rel_hbm, trap_hbm, out,
     c_in, f_in, rel_in, trap_in, factor, scale, partial, solved,
     rates, wide, levels, edge_out, edge_got,
-    load_sem, store_sem, edge_send, edge_recv, rate_send, rate_recv, halo_send, halo_recv,
+    load_sem, edge_send, edge_recv, rate_send, rate_recv, halo_send, halo_recv,
 ):
     blocks, planes, rows, lanes = c_in.shape
     chunks = planes // SUB
@@ -428,17 +428,11 @@
                 range(rows - 1 - inner, rows + reach - inner),
             ))
             if step == STEPS - 1:
-                for b in every:
-                    store(group, b).start()
+                for n in range(SUB):
+                    x = group * SUB + n
+                    for b in every:
+                        out[x, :, b * lanes:(b + 1) * lanes] = c_in[b, x]
             return carry
-
-        def store(group, b):
-            part = pl.ds(group * SUB, SUB)
-            return pltpu.make_async_copy(
-                c_in.at[b, part],
-                out_hbm.at[part, :, pl.ds(b * lanes, lanes)],
-                store_sem.at[group, b],
-            )
 
         lax.fori_loop(0, chunks, inside, 0)
         if step == 0:
@@ -451,9 +445,6 @@
     for step in range(STEPS):
         for k in range(chunks):
             sent_two(*halo_copies(step, k))
-    for group in range(chunks):
-        for b in every:
-            store(group, b).wait()
 
 
 def fused(concentration, face_conductance, release, trap_rate):
@@ -467,9 +458,9 @@
     )
     parts = pl.pallas_call(
         kernel,
-        out_shape=jax.ShapeDtypeStruct((planes, rows, depth), jnp.float32),
+        out_shape=pltpu.VMEM((planes, rows, depth), jnp.float32),
         in_specs=[pl.BlockSpec(memory_space=pl.ANY)] * 4,
-        out_specs=pl.BlockSpec(memory_space=pl.ANY),
+        out_specs=pl.BlockSpec(memory_space=pltpu.VMEM),
         scratch_shapes=[block] * 4 + [kept] * 3 + [block] + [
             pltpu.VMEM(
                 (2, rows + 2 * (SUBSTEPS - 1), chunks, blocks, SUB, LANES), jnp.float32
@@ -479,7 +470,6 @@
             ),
             stage, edge, edge,
             pltpu.SemaphoreType.DMA((4, blocks)),
-            pltpu.SemaphoreType.DMA((chunks, blocks)),
             pltpu.SemaphoreType.DMA((2,)),
             pltpu.SemaphoreType.DMA((2,)),
             pltpu.SemaphoreType.DMA((2,)),

time: 22.5 us -> 20.7 us (0.920)
  local copies, waits for them, and re-layouts: 1.87 us -> 0.8 us
  Pallas kernels: 20.4 us -> 19.7 us
    unnamed x1, local copies, waits for them, and re-layouts: 1.87 us -> 0.8 us
    pallas_call x1, Pallas kernels: 20.4 us -> 19.7 us  [fused(): pl.pallas_call(kernel, out_shape=pltpu.VMEM((planes, rows, depth), jnp.fl...]
where the time goes in v2:
time: 20.7 us; the launch traced here: 20.6 us
  Pallas kernels  19.7 us (95%)
  local copies, waits for them, and re-layouts  0.8 us (4%)
    pallas_call x1, Pallas kernels, fused(): pl.pallas_call(kernel, out_shape=pltpu.VMEM((planes, rows, depth), jnp.fl...  19.7 us
    unnamed x1, local copies, waits for them, and re-layouts  0.8 us

profile of v2, /device:TPU:1, one launch (start us, length us, event | category | flops | bytes accessed | tf_op | source)
XLA Modules:
  0.0 20.6 jit_solution(16137025728805171641)
XLA Ops:
  0.0 19.7 %shard_map.46 = f32[32,16,256]{2,1,0:T(8,128)S(1)} custom-call(f32[32,16,256]{2,1,0:T(8,128)} %c_hbm.1, f32[32,16,256]{2,1,0:T(8,128)} %f_hbm.1, f32[32,16,256]{2,1,0:T(8,128)} %rel_hbm.1, f32[32,16,256]{2,1,0:T(8,128)} %trap_hbm.1), custom_call_target="tpu_custom_call" | custom-call | tf_op jit(solution)/shard_map/pallas_call | solution.py:459
  19.8 0.8 %copy.6 = f32[32,16,256]{2,1,0:T(8,128)} copy(f32[32,16,256]{2,1,0:T(8,128)S(1)} %shard_map.46) | data formatting | bytes 1048576
